TPU v7x, 256 devices: a whole 4x4x8 slice. The times are simulated.
256 devices in a mesh: dp: 16 (over x, y), tensor: 16 (over z, core).
Axes of the slice: x: 4, y: 4, z: 8, core: 2. Of those that a mesh axis runs over, the one named last changes fastest.
Arguments:
- tokens: bfloat16 [32768, 1280], P(('dp', 'tensor'))
- cotangent: bfloat16 [32768, 1280], P(('dp', 'tensor')), may hold values from -6 to 6
- gate_weights: float32 [32768, 2], P(('dp', 'tensor')), may hold values from 0.2 to 1
- routes: int32 [32768, 2], P(('dp', 'tensor')), may hold values from 0 to 31, as said below
- slot_index: int32 [32768, 2], P(('dp', 'tensor')), may hold values from -1 to 1, as said below
- qkv_weight: bfloat16 [1280, 16, 240], P(None, 'tensor'), may hold values from -0.15625 to 0.15625
- proj_weight: bfloat16 [16, 80, 1280], P('tensor'), may hold values from -1.25 to 1.25
- up_weight: bfloat16 [32, 1280, 5120], P('dp', None, 'tensor'), may hold values from -0.15625 to 0.15625
- down_weight: bfloat16 [32, 5120, 1280], P('dp', 'tensor'), may hold values from -0.078125 to 0.078125
Outputs:
- layer_out: bfloat16 [32768, 1280], P(('dp', 'tensor'))
- gate_grad: float32 [32768, 2], P(('dp', 'tensor'))
- grad_qkv: float32 [1280, 16, 240], P('dp', 'tensor')
- grad_proj: float32 [16, 80, 1280], P('tensor', None, 'dp')
- grad_up: bfloat16 [32, 1280, 5120], P('dp', None, 'tensor')
- grad_down: bfloat16 [32, 5120, 1280], P('dp', 'tensor')
Inputs may be any that keep to these rules, and one draw needn't show every extreme that they name: `routes`: the two experts of a row differ. `slot_index`: -1 marks a dropped pair; within the rows of one device (aligned blocks of 128 rows) and one expert, the kept pairs hold the slots 0, 1, 2, ... without gaps, each at most once.
All inputs are finite; a program needn't handle non-finite values.
Results may differ from a plain program's by a relative error of at most 0.035.
Values may be sent and summed in bfloat16 or wider, within the bound.
A program may use at most 128 MiB of HBM per device.

v0:
```python
from functools import partial
import math
import jax
import jax.numpy as jnp
from jax import lax
from jax.sharding import PartitionSpec as P

CAP = 2
epsilon = 1e-06
half_root = 1.0 / math.sqrt(2.0)
bell_scale = 1.0 / math.sqrt(2.0 * math.pi)


def norm_parts(row_block):
    widened = row_block.astype(jnp.float32)
    center = widened - jnp.mean(widened, axis=-1, keepdims=True)
    factor = lax.rsqrt(jnp.mean(center * center, axis=-1, keepdims=True) + epsilon)
    return (center * factor, factor)


def norm_back(normal_rows, factor, upstream):
    mean_up = jnp.mean(upstream, axis=-1, keepdims=True)
    mean_mix = jnp.mean(upstream * normal_rows, axis=-1, keepdims=True)
    return factor * (upstream - mean_up - normal_rows * mean_mix)


def gelu_value(pre_act):
    return 0.5 * pre_act * (1.0 + lax.erf(pre_act * half_root))


def gelu_slope(pre_act):
    return (
        0.5 * (1.0 + lax.erf(pre_act * half_root))
        + pre_act * jnp.exp(-0.5 * pre_act * pre_act) * bell_scale
    )


def block_shares(query_block, key_rows, score_scale):
    scores = (
        jnp.einsum("qk,tk->qt", query_block, key_rows, preferred_element_type=jnp.float32)
        * score_scale
    )
    raised = jnp.exp(scores)
    return raised / jnp.sum(raised, axis=-1, keepdims=True)


def attend_head(queries, key_rows, value_rows, block_rows, score_scale):
    block_count = queries.shape[0] // block_rows

    def attend_one_block(query_block):
        shares = block_shares(query_block, key_rows, score_scale)
        context = jnp.dot(
            shares.astype(jnp.bfloat16), value_rows, preferred_element_type=jnp.float32
        )
        return context.astype(jnp.bfloat16)

    outputs = lax.map(attend_one_block, queries.reshape(block_count, block_rows, queries.shape[1]))
    return outputs.reshape(queries.shape)


def head_backward(queries, key_rows, value_rows, grad_context, block_rows, score_scale):
    block_count = queries.shape[0] // block_rows

    def head_one_block(carry, pieces):
        grad_keys, grad_values = carry
        query_block, grad_block = pieces
        shares = block_shares(query_block, key_rows, score_scale)
        grad_shares = jnp.einsum(
            "qk,tk->qt", grad_block, value_rows, preferred_element_type=jnp.float32
        )
        grad_scores = (
            shares
            * (grad_shares - jnp.sum(shares * grad_shares, axis=-1, keepdims=True))
            * score_scale
        ).astype(jnp.bfloat16)
        grad_query = jnp.dot(grad_scores, key_rows, preferred_element_type=jnp.float32).astype(
            jnp.bfloat16
        )
        grad_keys = grad_keys + jnp.einsum(
            "qt,qk->tk", grad_scores, query_block, preferred_element_type=jnp.float32
        )
        grad_values = grad_values + jnp.einsum(
            "qt,qk->tk", shares.astype(jnp.bfloat16), grad_block, preferred_element_type=jnp.float32
        )
        return ((grad_keys, grad_values), grad_query)

    zeros_rows = jnp.zeros(key_rows.shape, jnp.float32)
    shaped = (
        queries.reshape(block_count, block_rows, queries.shape[1]),
        grad_context.reshape(block_count, block_rows, queries.shape[1]),
    )
    (grad_keys, grad_values), grad_queries = lax.scan(
        head_one_block, (zeros_rows, zeros_rows), shaped
    )
    return (
        grad_queries.reshape(queries.shape),
        grad_keys.astype(jnp.bfloat16),
        grad_values.astype(jnp.bfloat16),
    )


def return_slots(expert_partial):
    summed = lax.psum_scatter(
        expert_partial.astype(jnp.bfloat16), "tensor", scatter_dimension=0, tiled=True
    ).astype(jnp.float32)
    returned = lax.all_to_all(
        summed[0].astype(jnp.bfloat16), "dp", split_axis=0, concat_axis=0, tiled=True
    )
    return returned.reshape(
        returned.shape[0] * returned.shape[1] * returned.shape[2], returned.shape[3]
    )


def shards(
    tokens,
    cotangent,
    gate_weights,
    routes,
    slot_index,
    qkv_weight,
    proj_weight,
    up_weight,
    down_weight,
):
    rows_dev, model_width = tokens.shape
    head_size = qkv_weight.shape[2] // 3
    score_scale = head_size ** (-0.5)
    group_count = lax.axis_size("dp")
    local_experts = up_weight.shape[0]
    places = group_count * local_experts * CAP
    normal_in, factor_in = norm_parts(tokens)
    normed = normal_in.astype(jnp.bfloat16)
    full_norm = lax.all_gather(normed, "tensor", axis=0, tiled=True)
    seq_len = full_norm.shape[0]
    block_rows = min(512, seq_len)
    qkv_rows = jnp.einsum(
        "sd,dhc->hsc", full_norm, qkv_weight, preferred_element_type=jnp.float32
    ).astype(jnp.bfloat16)
    queries = qkv_rows[:, :, :head_size]
    key_rows = qkv_rows[:, :, head_size : 2 * head_size]
    value_rows = qkv_rows[:, :, 2 * head_size :]
    context = jax.vmap(partial(attend_head, block_rows=block_rows, score_scale=score_scale))(
        queries, key_rows, value_rows
    )
    attention = lax.psum_scatter(
        jnp.einsum("hsk,hkd->sd", context, proj_weight, preferred_element_type=jnp.float32).astype(
            jnp.bfloat16
        ),
        "tensor",
        scatter_dimension=0,
        tiled=True,
    ).astype(jnp.float32)
    mid = (tokens.astype(jnp.float32) + attention).astype(jnp.bfloat16)
    normal_mid, factor_mid = norm_parts(mid)
    mid_normed = normal_mid.astype(jnp.bfloat16)
    slot_code = jnp.where(slot_index >= 0, routes * CAP + slot_index, -1)
    positions = jnp.arange(places, dtype=jnp.int32)
    pick_both = (slot_code[None, :, :] == positions[:, None, None]).astype(jnp.bfloat16)
    pick_first = pick_both[:, :, 0]
    pick_second = pick_both[:, :, 1]
    dispatch_rows = pick_first + pick_second
    outgoing = jnp.dot(dispatch_rows, mid_normed, preferred_element_type=jnp.float32).astype(
        jnp.bfloat16
    )
    outgoing = outgoing.reshape(group_count, local_experts, CAP, model_width)
    landed = lax.all_to_all(outgoing, "dp", split_axis=0, concat_axis=0, tiled=True)
    arrived = lax.all_gather(landed[None], "tensor", axis=0, tiled=True)
    pre_act = jnp.einsum("tsecd,edf->tsecf", arrived, up_weight, preferred_element_type=jnp.float32)
    hidden = gelu_value(pre_act).astype(jnp.bfloat16)
    expert_partial = jnp.einsum(
        "tsecf,efd->tsecd", hidden, down_weight, preferred_element_type=jnp.float32
    )
    returned = return_slots(expert_partial)
    expert_first = jnp.einsum("pr,pd->rd", pick_first, returned, preferred_element_type=jnp.float32)
    expert_second = jnp.einsum(
        "pr,pd->rd", pick_second, returned, preferred_element_type=jnp.float32
    )
    mixed_rows = gate_weights[:, 0:1] * expert_first + gate_weights[:, 1:2] * expert_second
    layer_out = (mid.astype(jnp.float32) + mixed_rows).astype(jnp.bfloat16)
    upstream = cotangent.astype(jnp.float32)
    gate_grad = jnp.stack(
        [jnp.sum(upstream * expert_first, axis=-1), jnp.sum(upstream * expert_second, axis=-1)],
        axis=1,
    )
    grad_first = (gate_weights[:, 0:1] * upstream).astype(jnp.bfloat16)
    grad_second = (gate_weights[:, 1:2] * upstream).astype(jnp.bfloat16)
    grad_outgoing = jnp.dot(pick_first, grad_first, preferred_element_type=jnp.float32) + jnp.dot(
        pick_second, grad_second, preferred_element_type=jnp.float32
    )
    grad_outgoing = grad_outgoing.astype(jnp.bfloat16).reshape(
        group_count, local_experts, CAP, model_width
    )
    grad_landed = lax.all_to_all(grad_outgoing, "dp", split_axis=0, concat_axis=0, tiled=True)
    grad_arrived = lax.all_gather(grad_landed[None], "tensor", axis=0, tiled=True)
    grad_hidden = jnp.einsum(
        "tsecd,efd->tsecf", grad_arrived, down_weight, preferred_element_type=jnp.float32
    )
    grad_pre = (grad_hidden * gelu_slope(pre_act)).astype(jnp.bfloat16)
    grad_down = jnp.einsum(
        "tsecf,tsecd->efd", hidden, grad_arrived, preferred_element_type=jnp.float32
    ).astype(jnp.bfloat16)
    grad_up = jnp.einsum(
        "tsecd,tsecf->edf", arrived, grad_pre, preferred_element_type=jnp.float32
    ).astype(jnp.bfloat16)
    grad_partial = jnp.einsum(
        "tsecf,edf->tsecd", grad_pre, up_weight, preferred_element_type=jnp.float32
    )
    grad_back = return_slots(grad_partial)
    grad_norm = jnp.einsum(
        "pr,pd->rd", dispatch_rows, grad_back, preferred_element_type=jnp.float32
    )
    grad_mid = (upstream + norm_back(normal_mid, factor_mid, grad_norm)).astype(jnp.bfloat16)
    full_grad = lax.all_gather(grad_mid, "tensor", axis=0, tiled=True)
    grad_context = jnp.einsum(
        "sd,hkd->hsk", full_grad, proj_weight, preferred_element_type=jnp.float32
    ).astype(jnp.bfloat16)
    grad_proj = jnp.einsum("hsk,sd->hkd", context, full_grad, preferred_element_type=jnp.float32)
    grad_queries, grad_keys, grad_values = jax.vmap(
        partial(head_backward, block_rows=block_rows, score_scale=score_scale)
    )(queries, key_rows, value_rows, grad_context)
    grad_rows = jnp.concatenate([grad_queries, grad_keys, grad_values], axis=-1)
    grad_qkv = jnp.einsum("sd,hsc->dhc", full_norm, grad_rows, preferred_element_type=jnp.float32)
    grad_qkv, grad_proj = (
        lax.psum_scatter(
            grad_qkv.astype(jnp.bfloat16), "dp", scatter_dimension=0, tiled=True
        ).astype(jnp.float32),
        lax.psum_scatter(
            grad_proj.astype(jnp.bfloat16), "dp", scatter_dimension=2, tiled=True
        ).astype(jnp.float32),
    )
    return (layer_out, gate_grad, grad_qkv, grad_proj, grad_up, grad_down)


def solution(mesh):
    return jax.shard_map(
        shards,
        mesh=mesh,
        in_specs=(
            P(("dp", "tensor"), None),
            P(("dp", "tensor"), None),
            P(("dp", "tensor"), None),
            P(("dp", "tensor"), None),
            P(("dp", "tensor"), None),
            P(None, "tensor", None),
            P("tensor", None, None),
            P("dp", None, "tensor"),
            P("dp", "tensor", None),
        ),
        out_specs=(
            P(("dp", "tensor"), None),
            P(("dp", "tensor"), None),
            P("dp", "tensor", None),
            P("tensor", None, "dp"),
            P("dp", None, "tensor"),
            P("dp", "tensor", None),
        ),
        check_vma=False,
    )
```

profile of v0, /device:TPU:2, one launch (start us, length us, event | category | flops | bytes accessed | tf_op | source)
XLA Modules:
  0.0 631.2 jit_solution(2711527637385925915)
XLA Ops:
  9.7 1.9 fusion.87
  11.7 46.4 %all-gather.7.cloned.1.call-done = bf16[2048,1280]{1,0:T(8,128)(2,1)} async-done(((bf16[128,1280]{1,0:T(8,128)(2,1)}), bf16[2048,1280]{1,0:T(8,128)(2,1)}) %all-gather.7.cloned.1.call-update) | async-done | bytes 5242896 | tf_op jit(solution)/shard_map/all_gather | solution.py:133
  58.0 4.2 fusion.47
  63.9 8.0 %while.25 = (s32[]{:T(128)}, bf16[4,1,512,80]{2,3,1,0:T(8,128)(2,1)S(1)}, bf16[4,1,512,80]{3,2,1,0:T(8,128)(2,1)S(1)}, bf16[1,2048,80]{2,1,0:T(8,128)(2,1)S(1)}, bf16[1,2048,80]{2,1,0:T(8,128)(2,1)}, /*index=5*/s32[]{:T(128)}) while((s32[]{:T(128)}, bf16[4,1,512,80]{2,3,1,0:T(8,128)(2,1)S(1)}, bf16[4,1,512,80]{3,2,1,0:T(8,128)(2,1)S(1)}, ...), condition=%wide.region_4.5_spmd, body=%wide.region_2.4_spmd.sunk | while | flops 340827648 | bytes 10965105 | solution.py:57
  72.3 3.9 convolution_convert_fusion.1
  77.6 62.2 %reduce-scatter.12.cloned.1.call-done = bf16[128,1280]{1,0:T(8,128)(2,1)} async-done(((bf16[2048,1280]{1,0:T(8,128)(2,1)}), bf16[128,1280]{1,0:T(8,128)(2,1)}) %reduce-scatter.12.cloned.1.call-update) | async-done | bytes 327696 | tf_op jit(solution)/shard_map/reduce_scatter | solution.py:145
  141.7 1.7 convolution_convert_fusion.8
  145.1 13.8 %all_to_all.20 = bf16[16,2,2,1280]{3,2,1,0:T(2,128)(2,1)S(1)} all-to-all(bf16[16,2,2,1280]{3,2,1,0:T(2,128)(2,1)} %reshape.172), channel_id=1, replica_groups=mesh['dp'=16,'tensor'=16] {'dp'}, dimensions={0} | all-to-all | bytes 327680 | tf_op jit(solution)/shard_map/all_to_all | solution.py:166
  161.7 1.7 fusion.48
  165.0 11.6 %all_to_all.21 = bf16[16,2,2,1280]{3,2,1,0:T(2,128)(2,1)S(1)} all-to-all(bf16[16,2,2,1280]{3,2,1,0:T(2,128)(2,1)} %reshape.174), channel_id=1, replica_groups=mesh['dp'=16,'tensor'=16] {'dp'}, dimensions={0} | all-to-all | bytes 327680 | tf_op jit(solution)/shard_map/all_to_all | solution.py:193
  177.5 19.0 %all-gather.11.cloned.1.call-done = bf16[256,2,2,1280]{3,0,2,1:T(8,128)(2,1)} async-done(((bf16[16,2,2,1280]{3,0,2,1:T(8,128)(2,1)}), bf16[256,2,2,1280]{3,0,2,1:T(8,128)(2,1)}) %all-gather.11.cloned.1.call-update) | async-done | bytes 2621456 | tf_op jit(solution)/shard_map/all_gather | solution.py:167
  196.6 4.7 fusion.62
  201.2 36.6 %all-gather.13.cloned.1.call-done = bf16[256,2,2,1280]{3,0,2,1:T(8,128)(2,1)} async-done(((bf16[16,2,2,1280]{3,0,2,1:T(8,128)(2,1)}), bf16[256,2,2,1280]{3,0,2,1:T(8,128)(2,1)}) %all-gather.13.cloned.1.call-update) | async-done | bytes 2621456 | tf_op jit(solution)/shard_map/all_gather | solution.py:194
  237.8 4.3 fusion.60
  243.0 3.0 fusion.38
  246.0 3.0 fusion.37
  250.3 122.9 %all-reduce.9.cloned.1.call-done = (bf16[16,16,2,2,1280]{4,1,3,0,2:T(8,128)(2,1)}, bf16[16,16,2,2,1280]{4,1,3,0,2:T(8,128)(2,1)}) async-done(((bf16[16,16,2,2,1280]{4,1,3,0,2:T(8,128)(2,1)}, bf16[16,16,2,2,1280]{4,1,3,0,2:T(8,128)(2,1)}), (bf16[16,16,2,2,1280]{4,1,3,0,2:T(8,128)(2,1)}, bf16[16,16,2,2,1280]{4,1,3,0,2:T(8,128)(2,1)})) %all-reduce.9.cloned.1.call-update) | async-done | bytes 5242896
  375.5 7.3 %all-to-all-start.3 = ((bf16[16,2,2,1280]{3,2,1,0:T(2,128)(2,1)}), bf16[16,2,2,1280]{3,2,1,0:T(2,128)(2,1)S(1)}, u32[]{:S(2)}, u32[]{:S(2)}) async-start(bf16[16,2,2,1280]{3,2,1,0:T(2,128)(2,1)} %copy.57), calls=%async_computation.4 | async-start | bytes 327680 | tf_op jit(solution)/shard_map/all_to_all | solution.py:106
  385.2 4.1 all-to-all-done.3
  389.3 5.1 all-to-all-start.1
  394.6 1.9 fusion.114
  396.5 4.4 all-to-all-done.1
  401.3 3.0 fusion.90
  406.3 4.0 fusion.40
  410.2 35.1 %all-gather.9.cloned.1.call-done = bf16[2048,1280]{1,0:T(8,128)(2,1)} async-done(((bf16[128,1280]{1,0:T(8,128)(2,1)}), bf16[2048,1280]{1,0:T(8,128)(2,1)}) %all-gather.9.cloned.1.call-update) | async-done | bytes 5242896 | tf_op jit(solution)/shard_map/all_gather | solution.py:213
  445.3 4.2 fusion.50
  449.8 4.2 fusion.49
  455.1 23.7 %while.26 = (s32[]{:T(128)}, f32[1,2048,80]{1,2,0:T(8,128)S(1)}, f32[1,2048,80]{1,2,0:T(8,128)S(1)}, bf16[4,1,512,80]{2,3,1,0:T(8,128)(2,1)S(1)}, bf16[4,1,512,8...) while((s32[]{:T(128)}, f32[1,2048,80]{1,2,0:T(8,128)S(1)}, ...), condition=%wide.region_17.18_spmd.clone, body=%wide.region_14.17_spmd.clone.sunk | while | flops 855284736 | bytes 37580964 | solution.py:92
  478.9 4.0 convolution_convert_fusion.4
  484.0 4.1 fusion.39
  488.7 52.8 %all-reduce.7.cloned.1.call-done = bf16[1,80,1280]{2,1,0:T(8,128)(2,1)} async-done(((bf16[1,80,1280]{2,1,0:T(8,128)(2,1)}), bf16[1,80,1280]{2,1,0:T(8,128)(2,1)}) %all-reduce.7.cloned.1.call-update) | async-done | bytes 204816
  543.0 79.8 %reduce-scatter.14.cloned.1.call-done = bf16[80,240]{1,0:T(8,128)(2,1)} async-done(((bf16[1280,240]{1,0:T(8,128)(2,1)}), bf16[80,240]{1,0:T(8,128)(2,1)}) %reduce-scatter.14.cloned.1.call-update) | async-done | bytes 38416
  (158 shorter events, 61.0 us)
Async XLA Ops:
  7.2 189.4 %copy-start = (bf16[2,1280,320]{1,2,0:T(8,128)(2,1)S(1)}, bf16[2,1280,320]{1,2,0:T(8,128)(2,1)}, u32[]{:S(2)}) copy-start(bf16[2,1280,320]{1,2,0:T(8,128)(2,1)} %param.20) | copy-start | bytes 4915204
  7.2 50.8 %all-gather.7.cloned.1.call-start = ((), (), s32[]{:S(2)}) async-start(), calls=%async_computation.6 | async-start | bytes 5570560 | tf_op jit(solution)/shard_map/all_gather | solution.py:133
  11.6 128.1 %reduce-scatter.12.cloned.1.call-start = ((), (), s32[]{:S(2)}) async-start(), calls=%async_computation.7 | async-start | bytes 5570560 | tf_op jit(solution)/shard_map/reduce_scatter | solution.py:145
  63.9 8.4 %copy-start.7 = (bf16[1,80,1280]{2,1,0:T(8,128)(2,1)S(1)}, bf16[1,80,1280]{2,1,0:T(8,128)(2,1)}, u32[]{:S(2)}) copy-start(bf16[1,80,1280]{2,1,0:T(8,128)(2,1)} %param.19) | copy-start | bytes 614404
  63.9 1.1 copy-start.13
  76.2 63.5 %copy-start.2 = (bf16[128,1280]{1,0:T(8,128)(2,1)S(1)}, bf16[128,1280]{1,0:T(8,128)(2,1)}, u32[]{:S(2)}) copy-start(bf16[128,1280]{1,0:T(8,128)(2,1)} %param.13) | copy-start | bytes 983044
  76.3 120.3 %all-gather.11.cloned.1.call-start = ((), (), s32[]{:S(2)}) async-start(), calls=%async_computation.9 | async-start | bytes 2785280 | tf_op jit(solution)/shard_map/all_gather | solution.py:167
  140.9 20.8 %copy-start.6 = (bf16[128,1280]{1,0:T(8,128)(2,1)S(1)}, bf16[128,1280]{1,0:T(8,128)(2,1)}, u32[]{:S(2)}) copy-start(bf16[128,1280]{1,0:T(8,128)(2,1)} %param.14) | copy-start | bytes 983044
  159.5 78.3 %all-gather.13.cloned.1.call-start = ((), (), s32[]{:S(2)}) async-start(), calls=%async_computation.10 | async-start | bytes 2785280 | tf_op jit(solution)/shard_map/all_gather | solution.py:194
  160.3 1.3 copy-start.17
  177.3 195.9 %all-reduce.9.cloned.1.call-start = ((), (), s32[]{:S(2)}) async-start(), calls=%async_computation.13 | async-start | bytes 10485760
  243.0 3.0 copy-start.5
  243.0 3.0 copy-start.8
  249.0 145.5 %copy-start.4 = (bf16[128,1280]{1,0:T(8,128)(2,1)S(1)}, bf16[128,1280]{1,0:T(8,128)(2,1)}, u32[]{:S(2)}) copy-start(bf16[128,1280]{1,0:T(8,128)(2,1)} %copy-done.3) | copy-start | bytes 983044
  249.0 145.5 %copy-start.22 = (f32[128]{0:T(128)S(1)}, f32[128]{0:T(128)}, u32[]{:S(2)}) copy-start(f32[128]{0:T(128)} %copy-done.21) | copy-start | bytes 1540
  249.1 151.9 %copy-start.16 = (pred[64,128,2]{1,0,2:T(32,128)(4,1)S(1)}, pred[64,128,2]{1,0,2:T(32,128)(4,1)}, u32[]{:S(2)}) copy-start(pred[64,128,2]{1,0,2:T(32,128)(4,1)} %get-tuple-element.212) | copy-start | bytes 49156
  249.1 152.2 %copy-start.18 = (f32[128]{0:T(128)S(1)}, f32[128]{0:T(128)}, u32[]{:S(2)}) copy-start(f32[128]{0:T(128)} %copy-done.17) | copy-start | bytes 1540
  375.5 13.7 %all-to-all-start.3 = ((bf16[16,2,2,1280]{3,2,1,0:T(2,128)(2,1)}), bf16[16,2,2,1280]{3,2,1,0:T(2,128)(2,1)S(1)}, u32[]{:S(2)}, u32[]{:S(2)}) async-start(bf16[16,2,2,1280]{3,2,1,0:T(2,128)(2,1)} %copy.57), calls=%async_computation.4 | async-start | bytes 327680 | tf_op jit(solution)/shard_map/all_to_all | solution.py:106
  389.3 11.6 %all-to-all-start.1 = ((bf16[16,2,2,1280]{3,2,1,0:T(2,128)(2,1)}), bf16[16,2,2,1280]{3,2,1,0:T(2,128)(2,1)S(1)}, u32[]{:S(2)}, u32[]{:S(2)}) async-start(bf16[16,2,2,1280]{3,2,1,0:T(2,128)(2,1)} %copy.54), calls=%async_computation.2 | async-start | bytes 327680 | tf_op jit(solution)/shard_map/all_to_all | solution.py:106
  394.4 50.9 %all-gather.9.cloned.1.call-start = ((), (), s32[]{:S(2)}) async-start(), calls=%async_computation.8 | async-start | bytes 5570560 | tf_op jit(solution)/shard_map/all_gather | solution.py:213
  394.6 11.7 %copy-start.11 = (bf16[16,16,2,2,320]{4,1,3,0,2:T(8,128)(2,1)S(1)}, bf16[16,16,2,2,320]{4,1,3,0,2:T(8,128)(2,1)}, u32[]{:S(2)}) copy-start(bf16[16,16,2,2,320]{4,1,3,0,2:T(8,128)(2,1)} %copy-done.10) | copy-start | bytes 1966084
  404.3 137.2 %all-reduce.7.cloned.1.call-start = ((), (), s32[]{:S(2)}) async-start(), calls=%async_computation.12 | async-start | bytes 409600
  449.5 5.6 copy-start.12
  449.5 5.6 copy-start.14
  449.5 173.2 %reduce-scatter.14.cloned.1.call-start = ((), (), s32[]{:S(2)}) async-start(), calls=%async_computation.11 | async-start | bytes 696320
  455.1 1.0 copy-start.15
  461.0 1.0 copy-start.15
  466.9 1.0 copy-start.15
  478.9 5.1 copy-start.9
  484.0 4.1 copy-start.23
  484.0 4.1 copy-start.24
  484.0 140.4 %copy-start.1 = (bf16[2,1280,320]{1,2,0:T(8,128)(2,1)S(1)}, bf16[2,1280,320]{1,2,0:T(8,128)(2,1)}, u32[]{:S(2)}) copy-start(bf16[2,1280,320]{1,2,0:T(8,128)(2,1)} %param.20) | copy-start | bytes 4915204
  (10 other events, 8.4 us)
Sparse Core Ops, SparseCore 0:
  11.7 46.2 all-gather.6
  76.4 63.3 reduce-scatter.11
  159.6 36.8 all-gather.10
  198.8 38.9 all-gather.12
  249.2 123.9 all-reduce.8
  404.4 40.8 all-gather.8
  449.6 91.7 all-reduce.6
  545.4 77.3 reduce-scatter.13
where the time goes:
time: 633 us; the launch traced here: 631 us
  waiting for transfers between devices  463 us (73%)
  matrix products  78.8 us (12%)
  blocking collectives  25.4 us (4%)
  local copies, waits for them, and re-layouts  22.2 us (4%)
  between operations  15.2 us (2%)
  starting transfers between devices  13.1 us (2%)
  other arithmetic  13 us (2%)
    unnamed x11, waiting for transfers between devices  256 us
    reduce_scatter x1, waiting for transfers between devices, shards(): lax.psum_scatter(jnp.einsum('hsk,hkd->sd', context, proj_weight, preferre...  62.2 us
    all_gather x1, waiting for transfers between devices, shards(): full_norm = lax.all_gather(normed, 'tensor', axis=0, tiled=True)  46.4 us
    all_gather x1, waiting for transfers between devices, shards(): lax.all_gather(grad_landed[None], 'tensor', axis=0, tiled=True)  36.6 us
    all_gather x1, waiting for transfers between devices, shards(): full_grad = lax.all_gather(grad_mid, 'tensor', axis=0, tiled=True)  35.1 us
    all_gather x1, waiting for transfers between devices, shards(): arrived = lax.all_gather(landed[None], 'tensor', axis=0, tiled=True)  19 us
    all_to_all x1, blocking collectives, shards(): lax.all_to_all(outgoing, 'dp', split_axis=0, concat_axis=0, tiled=True)  13.8 us
  transfers between devices with their start and end apart: 10, of which 10 were waited for; matrix products, arithmetic and copies ran while one was open for 10% of the time, Pallas kernels for 0%

commit v1 on v0

--- a/solution.py
+++ b/solution.py
@@ -210,7 +210,9 @@
         "pr,pd->rd", dispatch_rows, grad_back, preferred_element_type=jnp.float32
     )
     grad_mid = (upstream + norm_back(normal_mid, factor_mid, grad_norm)).astype(jnp.bfloat16)
-    full_grad = lax.all_gather(grad_mid, "tensor", axis=0, tiled=True)
+    full_grad = jnp.concatenate(
+        lax.all_to_all(jnp.stack([grad_mid] * lax.axis_size("tensor")), "tensor", 0, 0), axis=0
+    )
     grad_context = jnp.einsum(
         "sd,hkd->hsk", full_grad, proj_weight, preferred_element_type=jnp.float32
     ).astype(jnp.bfloat16)

time: 633 us -> 718 us (1.13)
  waiting for transfers between devices: 463 us -> 544 us
    all_to_all x0 -> x1, waiting for transfers between devices: none -> 111 us  [shards(): lax.all_to_all(jnp.stack([grad_mid] * lax.axis_size('tensor')), 'tensor',...]
    all_gather x1 -> x0, waiting for transfers between devices: 35.1 us -> none  [shards(): full_grad = lax.all_gather(grad_mid, 'tensor', axis=0, tiled=True)]
    unnamed x11 -> x10, waiting for transfers between devices: 256 us -> 258 us
  transfers between devices with their start and end apart: 10 -> 10, of which waited for: 10 -> 10; matrix products, arithmetic and copies ran while one was open for 10% -> 8% of each run, Pallas kernels for 0% -> 0%
where the time goes in v1:
time: 718 us; the launch traced here: 717 us
  waiting for transfers between devices  544 us (76%)
  matrix products  76.2 us (11%)
  blocking collectives  25.3 us (4%)
  local copies, waits for them, and re-layouts  24.3 us (3%)
  starting transfers between devices  18.8 us (3%)
  between operations  15.2 us (2%)
  other arithmetic  13 us (2%)
    unnamed x10, waiting for transfers between devices  258 us
    all_to_all x1, waiting for transfers between devices, shards(): lax.all_to_all(jnp.stack([grad_mid] * lax.axis_size('tensor')), 'tensor',...  111 us
    reduce_scatter x1, waiting for transfers between devices, shards(): lax.psum_scatter(jnp.einsum('hsk,hkd->sd', context, proj_weight, preferre...  62.2 us
    all_gather x1, waiting for transfers between devices, shards(): full_norm = lax.all_gather(normed, 'tensor', axis=0, tiled=True)  46.4 us
    all_gather x1, waiting for transfers between devices, shards(): lax.all_gather(grad_landed[None], 'tensor', axis=0, tiled=True)  36.6 us
    all_gather x1, waiting for transfers between devices, shards(): arrived = lax.all_gather(landed[None], 'tensor', axis=0, tiled=True)  19 us
  transfers between devices with their start and end apart: 10, of which 10 were waited for; matrix products, arithmetic and copies ran while one was open for 8% of the time, Pallas kernels for 0%

profile of v1, /device:TPU:2, one launch (start us, length us, event | category | flops | bytes accessed | tf_op | source)
XLA Modules:
  0.0 716.7 jit_solution(8876604840972868410)
XLA Ops:
  9.7 1.9 fusion.87
  11.7 46.4 %all-gather.6.cloned.1.call-done = bf16[2048,1280]{1,0:T(8,128)(2,1)} async-done(((bf16[128,1280]{1,0:T(8,128)(2,1)}), bf16[2048,1280]{1,0:T(8,128)(2,1)}) %all-gather.6.cloned.1.call-update) | async-done | bytes 5242896 | tf_op jit(solution)/shard_map/all_gather | solution.py:133
  58.0 4.2 fusion.47
  63.9 8.0 %while.25 = (s32[]{:T(128)}, bf16[4,1,512,80]{2,3,1,0:T(8,128)(2,1)S(1)}, bf16[4,1,512,80]{3,2,1,0:T(8,128)(2,1)S(1)}, bf16[1,2048,80]{2,1,0:T(8,128)(2,1)S(1)}, bf16[1,2048,80]{2,1,0:T(8,128)(2,1)}, /*index=5*/s32[]{:T(128)}) while((s32[]{:T(128)}, bf16[4,1,512,80]{2,3,1,0:T(8,128)(2,1)S(1)}, bf16[4,1,512,80]{3,2,1,0:T(8,128)(2,1)S(1)}, ...), condition=%wide.region_4.5_spmd, body=%wide.region_2.4_spmd.sunk | while | flops 340827648 | bytes 10965105 | solution.py:57
  72.3 4.0 convolution_convert_fusion.1
  77.6 62.2 %reduce-scatter.12.cloned.1.call-done = bf16[128,1280]{1,0:T(8,128)(2,1)} async-done(((bf16[2048,1280]{1,0:T(8,128)(2,1)}), bf16[128,1280]{1,0:T(8,128)(2,1)}) %reduce-scatter.12.cloned.1.call-update) | async-done | bytes 327696 | tf_op jit(solution)/shard_map/reduce_scatter | solution.py:145
  141.7 1.7 convolution_convert_fusion.8
  145.1 13.7 %all_to_all.25 = bf16[16,2,2,1280]{3,2,1,0:T(2,128)(2,1)S(1)} all-to-all(bf16[16,2,2,1280]{3,2,1,0:T(2,128)(2,1)} %reshape.177), channel_id=1, replica_groups=mesh['dp'=16,'tensor'=16] {'dp'}, dimensions={0} | all-to-all | bytes 327680 | tf_op jit(solution)/shard_map/all_to_all | solution.py:166
  165.0 11.6 %all_to_all.26 = bf16[16,2,2,1280]{3,2,1,0:T(2,128)(2,1)S(1)} all-to-all(bf16[16,2,2,1280]{3,2,1,0:T(2,128)(2,1)} %reshape.179), channel_id=1, replica_groups=mesh['dp'=16,'tensor'=16] {'dp'}, dimensions={0} | all-to-all | bytes 327680 | tf_op jit(solution)/shard_map/all_to_all | solution.py:193
  177.5 19.0 %all-gather.8.cloned.1.call-done = bf16[256,2,2,1280]{3,0,2,1:T(8,128)(2,1)} async-done(((bf16[16,2,2,1280]{3,0,2,1:T(8,128)(2,1)}), bf16[256,2,2,1280]{3,0,2,1:T(8,128)(2,1)}) %all-gather.8.cloned.1.call-update) | async-done | bytes 2621456 | tf_op jit(solution)/shard_map/all_gather | solution.py:167
  196.5 4.7 fusion.62
  201.2 36.6 %all-gather.10.cloned.1.call-done = bf16[256,2,2,1280]{3,0,2,1:T(8,128)(2,1)} async-done(((bf16[16,2,2,1280]{3,0,2,1:T(8,128)(2,1)}), bf16[256,2,2,1280]{3,0,2,1:T(8,128)(2,1)}) %all-gather.10.cloned.1.call-update) | async-done | bytes 2621456 | tf_op jit(solution)/shard_map/all_gather | solution.py:194
  237.8 4.3 fusion.60
  243.0 3.0 fusion.38
  246.0 3.1 fusion.37
  250.4 122.9 %all-reduce.9.cloned.1.call-done = (bf16[16,16,2,2,1280]{4,1,3,0,2:T(8,128)(2,1)}, bf16[16,16,2,2,1280]{4,1,3,0,2:T(8,128)(2,1)}) async-done(((bf16[16,16,2,2,1280]{4,1,3,0,2:T(8,128)(2,1)}, bf16[16,16,2,2,1280]{4,1,3,0,2:T(8,128)(2,1)}), (bf16[16,16,2,2,1280]{4,1,3,0,2:T(8,128)(2,1)}, bf16[16,16,2,2,1280]{4,1,3,0,2:T(8,128)(2,1)})) %all-reduce.9.cloned.1.call-update) | async-done | bytes 5242896
  375.7 7.3 %all-to-all-start.3 = ((bf16[16,2,2,1280]{3,2,1,0:T(2,128)(2,1)}), bf16[16,2,2,1280]{3,2,1,0:T(2,128)(2,1)S(1)}, u32[]{:S(2)}, u32[]{:S(2)}) async-start(bf16[16,2,2,1280]{3,2,1,0:T(2,128)(2,1)} %copy.57), calls=%async_computation.4 | async-start | bytes 327680 | tf_op jit(solution)/shard_map/all_to_all | solution.py:106
  385.3 4.1 all-to-all-done.3
  389.4 5.1 all-to-all-start.1
  395.0 6.0 all-to-all-done.1
  401.4 1.7 fusion.90
  403.2 2.8 stack.11
  406.0 5.7 all-to-all-start.4
  413.0 4.0 fusion.40
  417.0 111.5 %all-to-all-done.4 = bf16[16,128,1280]{2,1,0:T(8,128)(2,1)} async-done(((bf16[16,128,1280]{2,1,0:T(8,128)(2,1)}), bf16[16,128,1280]{2,1,0:T(8,128)(2,1)}, u32[]{:S(2)}, u32[]{:S(2)}) %all-to-all-start.4) | async-done | bytes 5242912 | tf_op jit(solution)/shard_map/all_to_all | solution.py:214
  528.5 4.2 fusion.50
  532.7 4.3 fusion.49
  538.3 23.7 %while.26 = (s32[]{:T(128)}, f32[1,2048,80]{1,2,0:T(8,128)S(1)}, f32[1,2048,80]{1,2,0:T(8,128)S(1)}, bf16[4,1,512,80]{2,3,1,0:T(8,128)(2,1)S(1)}, bf16[4,1,512,8...) while((s32[]{:T(128)}, f32[1,2048,80]{1,2,0:T(8,128)S(1)}, ...), condition=%wide.region_17.18_spmd.clone, body=%wide.region_14.17_spmd.clone.sunk | while | flops 855284736 | bytes 37580964 | solution.py:92
  562.1 4.0 convolution_convert_fusion.4
  567.2 4.1 fusion.39
  571.9 55.1 %all-reduce.7.cloned.1.call-done = bf16[1,80,1280]{2,1,0:T(8,128)(2,1)} async-done(((bf16[1,80,1280]{2,1,0:T(8,128)(2,1)}), bf16[1,80,1280]{2,1,0:T(8,128)(2,1)}) %all-reduce.7.cloned.1.call-update) | async-done | bytes 204816
  628.5 79.8 %reduce-scatter.14.cloned.1.call-done = bf16[80,240]{1,0:T(8,128)(2,1)} async-done(((bf16[1280,240]{1,0:T(8,128)(2,1)}), bf16[80,240]{1,0:T(8,128)(2,1)}) %reduce-scatter.14.cloned.1.call-update) | async-done | bytes 38416
  (162 shorter events, 62.3 us)
Async XLA Ops:
  7.2 189.4 %copy-start = (bf16[2,1280,320]{1,2,0:T(8,128)(2,1)S(1)}, bf16[2,1280,320]{1,2,0:T(8,128)(2,1)}, u32[]{:S(2)}) copy-start(bf16[2,1280,320]{1,2,0:T(8,128)(2,1)} %param.20) | copy-start | bytes 4915204
  7.2 50.8 %all-gather.6.cloned.1.call-start = ((), (), s32[]{:S(2)}) async-start(), calls=%async_computation.7 | async-start | bytes 5570560 | tf_op jit(solution)/shard_map/all_gather | solution.py:133
  11.6 128.2 %reduce-scatter.12.cloned.1.call-start = ((), (), s32[]{:S(2)}) async-start(), calls=%async_computation.8 | async-start | bytes 5570560 | tf_op jit(solution)/shard_map/reduce_scatter | solution.py:145
  63.9 8.4 %copy-start.7 = (bf16[1,80,1280]{2,1,0:T(8,128)(2,1)S(1)}, bf16[1,80,1280]{2,1,0:T(8,128)(2,1)}, u32[]{:S(2)}) copy-start(bf16[1,80,1280]{2,1,0:T(8,128)(2,1)} %param.19) | copy-start | bytes 614404
  63.9 1.1 copy-start.13
  76.2 63.5 %copy-start.2 = (bf16[128,1280]{1,0:T(8,128)(2,1)S(1)}, bf16[128,1280]{1,0:T(8,128)(2,1)}, u32[]{:S(2)}) copy-start(bf16[128,1280]{1,0:T(8,128)(2,1)} %param.13) | copy-start | bytes 983044
  76.3 120.3 %all-gather.8.cloned.1.call-start = ((), (), s32[]{:S(2)}) async-start(), calls=%async_computation.9 | async-start | bytes 2785280 | tf_op jit(solution)/shard_map/all_gather | solution.py:167
  140.9 20.7 %copy-start.6 = (bf16[128,1280]{1,0:T(8,128)(2,1)S(1)}, bf16[128,1280]{1,0:T(8,128)(2,1)}, u32[]{:S(2)}) copy-start(bf16[128,1280]{1,0:T(8,128)(2,1)} %param.14) | copy-start | bytes 983044
  159.5 78.3 %all-gather.10.cloned.1.call-start = ((), (), s32[]{:S(2)}) async-start(), calls=%async_computation.10 | async-start | bytes 2785280 | tf_op jit(solution)/shard_map/all_gather | solution.py:194
  160.3 1.3 copy-start.18
  177.3 196.0 %all-reduce.9.cloned.1.call-start = ((), (), s32[]{:S(2)}) async-start(), calls=%async_computation.13 | async-start | bytes 10485760
  243.0 3.0 copy-start.5
  243.0 3.0 copy-start.8
  249.1 145.5 %copy-start.4 = (bf16[128,1280]{1,0:T(8,128)(2,1)S(1)}, bf16[128,1280]{1,0:T(8,128)(2,1)}, u32[]{:S(2)}) copy-start(bf16[128,1280]{1,0:T(8,128)(2,1)} %copy-done.3) | copy-start | bytes 983044
  249.1 145.5 %copy-start.17 = (bf16[64,128,2]{1,0,2:T(8,128)(2,1)S(1)}, bf16[64,128,2]{1,0,2:T(8,128)(2,1)}, u32[]{:S(2)}) copy-start(bf16[64,128,2]{1,0,2:T(8,128)(2,1)} %get-tuple-element.213) | copy-start | bytes 98308
  249.1 145.5 %copy-start.23 = (f32[128]{0:T(128)S(1)}, f32[128]{0:T(128)}, u32[]{:S(2)}) copy-start(f32[128]{0:T(128)} %copy-done.22) | copy-start | bytes 1540
  249.2 151.9 %copy-start.16 = (pred[64,128,2]{1,0,2:T(32,128)(4,1)S(1)}, pred[64,128,2]{1,0,2:T(32,128)(4,1)}, u32[]{:S(2)}) copy-start(pred[64,128,2]{1,0,2:T(32,128)(4,1)} %get-tuple-element.212) | copy-start | bytes 49156
  249.2 152.2 %copy-start.19 = (f32[128]{0:T(128)S(1)}, f32[128]{0:T(128)}, u32[]{:S(2)}) copy-start(f32[128]{0:T(128)} %copy-done.18) | copy-start | bytes 1540
  375.7 13.7 %all-to-all-start.3 = ((bf16[16,2,2,1280]{3,2,1,0:T(2,128)(2,1)}), bf16[16,2,2,1280]{3,2,1,0:T(2,128)(2,1)S(1)}, u32[]{:S(2)}, u32[]{:S(2)}) async-start(bf16[16,2,2,1280]{3,2,1,0:T(2,128)(2,1)} %copy.57), calls=%async_computation.4 | async-start | bytes 327680 | tf_op jit(solution)/shard_map/all_to_all | solution.py:106
  389.4 11.6 %all-to-all-start.1 = ((bf16[16,2,2,1280]{3,2,1,0:T(2,128)(2,1)}), bf16[16,2,2,1280]{3,2,1,0:T(2,128)(2,1)S(1)}, u32[]{:S(2)}, u32[]{:S(2)}) async-start(bf16[16,2,2,1280]{3,2,1,0:T(2,128)(2,1)} %copy.54), calls=%async_computation.2 | async-start | bytes 327680 | tf_op jit(solution)/shard_map/all_to_all | solution.py:106
  406.0 5.8 copy-start.26
  406.0 7.0 copy-start.11
  406.0 122.4 %all-to-all-start.4 = ((bf16[16,128,1280]{2,1,0:T(8,128)(2,1)}), bf16[16,128,1280]{2,1,0:T(8,128)(2,1)}, u32[]{:S(2)}, u32[]{:S(2)}) async-start(bf16[16,128,1280]{2,1,0:T(8,128)(2,1)} %stack.11), calls=%async_computation.5 | async-start | bytes 10485760 | tf_op jit(solution)/shard_map/all_to_all | solution.py:214
  411.7 215.3 %all-reduce.7.cloned.1.call-start = ((), (), s32[]{:S(2)}) async-start(), calls=%async_computation.12 | async-start | bytes 409600
  532.7 5.6 copy-start.12
  532.7 5.6 copy-start.14
  537.0 171.3 %reduce-scatter.14.cloned.1.call-start = ((), (), s32[]{:S(2)}) async-start(), calls=%async_computation.11 | async-start | bytes 696320
  544.2 1.0 copy-start.15
  562.1 5.1 copy-start.9
  567.2 4.1 copy-start.24
  567.2 4.1 copy-start.25
  567.2 142.7 %copy-start.1 = (bf16[2,1280,320]{1,2,0:T(8,128)(2,1)S(1)}, bf16[2,1280,320]{1,2,0:T(8,128)(2,1)}, u32[]{:S(2)}) copy-start(bf16[2,1280,320]{1,2,0:T(8,128)(2,1)} %param.20) | copy-start | bytes 4915204
  (12 other events, 10.4 us)
Sparse Core Ops, SparseCore 0:
  11.7 46.2 all-gather.5
  76.4 63.3 reduce-scatter.11
  159.6 36.8 all-gather.7
  198.8 38.9 all-gather.9
  249.3 123.9 all-reduce.8
  537.1 89.8 all-reduce.6
  630.9 77.3 reduce-scatter.13
